TPU v7x, 32 devices: a whole 2x2x4 slice. The times are simulated.
32 devices in a mesh: gx: 4 (over z), gy: 4 (over x, core), gz: 2 (over y).
Axes of the slice: x: 2, y: 2, z: 4, core: 2. Of those that a mesh axis runs over, the one named last changes fastest.
Arguments:
- features: float32 [4, 4, 2, 256, 256], P('gx', 'gy', 'gz'), may hold values from -6 to 6
- positions: float32 [4, 4, 2, 3, 256], P('gx', 'gy', 'gz'), may hold values from 0 to 1
- counts: int32 [4, 4, 2], P('gx', 'gy', 'gz'), may hold values from 51 to 256, as said below
- w_src: float32 [256, 256], replicated, may hold values from -0.375 to 0.375
- w_out: float32 [256, 256], replicated, may hold values from -0.375 to 0.375
- radial: float32 [8, 256], replicated, may hold values from -5 to 5
Outputs:
- updated: float32 [4, 4, 2, 256, 256], P('gx', 'gy', 'gz')
Inputs may be any that keep to these rules, and one draw needn't show every extreme that they name: The atoms of a bin fill its first counts slots; some bin is full in every draw, and some bins hold more than 128 atoms.
All inputs are finite; a program needn't handle non-finite values.
Results may differ from a plain program's by a relative error of at most 0.0003.
Values sent between devices are 32-bit elements; how exact they have to be, the bound alone decides.
A program may use at most 64 MiB of HBM per device.

v0:
```python
import jax
import jax.numpy as jnp
from jax import lax
from jax.sharding import PartitionSpec as P

NRBF = 8
CAP = 256
BLK = 128


far_value = 100.0
half_far = 50.0
gamma_width = 10.0
message_scale = 0.125
highest = lax.Precision.HIGHEST


def padded(cells, sides, width):
    for axis, dim in sides:
        count = lax.axis_size(axis)
        head = lax.slice_in_dim(cells, 0, width, axis=dim)
        tail = lax.slice_in_dim(cells, cells.shape[dim] - width, cells.shape[dim], axis=dim)
        cells = jnp.concatenate(
            [
                lax.ppermute(tail, axis, [(i, (i + 1) % count) for i in range(count)]),
                cells,
                lax.ppermute(head, axis, [((i + 1) % count, i) for i in range(count)]),
            ],
            axis=dim,
        )
    return cells


def offset_of(task_index):
    return (
        jnp.stack([task_index // 9, task_index // 3 % 3, task_index % 3]).astype(jnp.float32) - 1.0
    )


def radial_terms(left_pos, right_pos, right_feats, offset, same_bin, row_block, col_block, radial):
    rows_left = lax.dynamic_slice_in_dim(left_pos, row_block * BLK, BLK, 1)
    rows_right = lax.dynamic_slice_in_dim(right_pos, col_block * BLK, BLK, 1) + offset[:, None]
    separation = rows_right[:, None, :] - rows_left[:, :, None]
    distance = jnp.sqrt(jnp.sum(separation * separation, axis=0))
    envelope = jnp.where(distance < 1.0, 0.5 * (jnp.cos(jnp.pi * distance) + 1.0), 0.0)
    diagonal = lax.broadcasted_iota(jnp.int32, (BLK, BLK), 0) == lax.broadcasted_iota(
        jnp.int32, (BLK, BLK), 1
    )
    envelope = jnp.where(diagonal & same_bin & (row_block == col_block), 0.0, envelope)
    centres = (lax.broadcasted_iota(jnp.float32, (1, NRBF, 1), 1) + 0.5) / NRBF
    radial_basis = envelope[:, None, :] * jnp.exp(
        -gamma_width * (distance[:, None, :] - centres) ** 2
    )
    feature_rows = lax.dynamic_slice_in_dim(right_feats, col_block * BLK, BLK, 0)
    weighted = (radial[:, None, :] * feature_rows[None, :, :]).reshape(
        NRBF * BLK, feature_rows.shape[1]
    )
    return jnp.dot(
        radial_basis.reshape(BLK, NRBF * BLK),
        weighted,
        precision=highest,
        preferred_element_type=jnp.float32,
    )


def task_sum(
    left_pos, right_pos, right_feats, offset, same_bin, left_blocks, right_blocks, radial, running
):
    divisor = jnp.maximum(right_blocks, 1)

    def add_pair(counter, partial_sum):
        row_block = counter // divisor
        col_block = counter % divisor
        term = radial_terms(
            left_pos, right_pos, right_feats, offset, same_bin, row_block, col_block, radial
        )
        current = lax.dynamic_slice_in_dim(partial_sum, row_block * BLK, BLK, 0)
        return lax.dynamic_update_slice_in_dim(partial_sum, current + term, row_block * BLK, 0)

    return lax.fori_loop(0, left_blocks * right_blocks, add_pair, running)


def live_blocks(placed):
    return jnp.sum((placed[0, ::BLK] < half_far).astype(jnp.int32))


def pack_bin(feats, coords):
    joined = jnp.concatenate([feats.reshape(-1), coords.reshape(-1)])
    return joined[None, None, None]


def unpack_bins(joined, rows, width):
    flat = joined.reshape(27, -1)
    feats = flat[:, : rows * width].reshape(27, rows, width)
    coords = flat[:, rows * width :].reshape(27, 3, rows)
    return (feats, coords)


def local(features, positions, counts, w_src, w_out, radial):
    own_feats = features[0, 0, 0]
    width = own_feats.shape[1]
    projected = jnp.dot(own_feats, w_src, precision=highest, preferred_element_type=jnp.float32)
    slot_index = lax.broadcasted_iota(jnp.int32, (1, CAP), 1)
    placed = jnp.where(slot_index < counts[0, 0, 0], positions[0, 0, 0], far_value)
    early = padded(pack_bin(projected[:BLK], placed[:, :BLK]), (("gx", 0), ("gy", 1), ("gz", 2)), 1)
    later = padded(pack_bin(projected[BLK:], placed[:, BLK:]), (("gx", 0), ("gy", 1), ("gz", 2)), 1)
    early_feats, early_pos = unpack_bins(early, BLK, width)
    later_feats, later_pos = unpack_bins(later, CAP - BLK, width)
    near_feats = jnp.concatenate([early_feats, later_feats], axis=1)
    near_pos = jnp.concatenate([early_pos, later_pos], axis=2)
    own_blocks = live_blocks(placed)
    near_blocks = jnp.sum((near_pos[:, 0, ::BLK] < half_far).astype(jnp.int32), axis=1)
    running = jnp.zeros((CAP, width), jnp.float32)
    skipped = jnp.int32(0)

    def add_task(task_index, partial_sum):
        right_blocks = jnp.where(task_index < skipped, 0, near_blocks[task_index])
        return task_sum(
            placed,
            near_pos[task_index],
            near_feats[task_index],
            offset_of(task_index),
            task_index == 13,
            own_blocks,
            right_blocks,
            radial,
            partial_sum,
        )

    message = lax.fori_loop(0, 27, add_task, running)
    mixed = jnp.dot(
        message_scale * message, w_out, precision=highest, preferred_element_type=jnp.float32
    )
    return (own_feats + jax.nn.silu(mixed))[None, None, None]


def solution(mesh):
    in_specs = (
        P("gx", "gy", "gz", None, None),
        P("gx", "gy", "gz", None, None),
        P("gx", "gy", "gz"),
        P(),
        P(),
        P(),
    )
    out_specs = P("gx", "gy", "gz", None, None)
    return jax.shard_map(local, mesh=mesh, in_specs=in_specs, out_specs=out_specs, check_vma=False)
```

profile of v0, /device:TPU:14, one launch (start us, length us, event | category | flops | bytes accessed | tf_op | source)
XLA Modules:
  0.0 360.7 jit_solution(6334532601876277498)
XLA Ops:
  1.4 1.3 fusion.18
  3.5 1.6 collective-permute-start.6
  5.2 2.1 collective-permute-start.1
  8.1 6.2 %collective-permute-done.6 = f32[1,1,1,33152]{3,2,1,0:T(1,128)S(1)} collective-permute-done((f32[1,1,1,33152]{3,2,1,0:T(1,128)S(1)}, f32[1,1,1,33152]{3,2,1,0:T(1,128)S(1)}, u32[]{:S(2)}, u32[]{:S(2)}) %collective-permute-start.6) | collective-permute-done | bytes 132640 | tf_op jit(solution)/shard_map/ppermute | solution.py:25
  15.0 3.9 %collective-permute-done = f32[1,1,1,33152]{3,2,1,0:T(1,128)S(1)} collective-permute-done((f32[1,1,1,33152]{3,2,1,0:T(1,128)S(1)}, f32[1,1,1,33152]{3,2,1,0:T(1,128)S(1)}, u32[]{:S(2)}, u32[]{:S(2)}) %collective-permute-start) | collective-permute-done | bytes 132640 | tf_op jit(solution)/shard_map/ppermute | solution.py:25
  19.6 4.5 %collective-permute-done.9 = f32[3,1,1,33152]{3,2,1,0:T(1,128)S(1)} collective-permute-done((f32[3,1,1,33152]{3,2,1,0:T(1,128)S(1)}, f32[3,1,1,33152]{3,2,1,0:T(1,128)S(1)}, u32[]{:S(2)}, u32[]{:S(2)}) %collective-permute-start.9) | collective-permute-done | bytes 397856 | tf_op jit(solution)/shard_map/ppermute | solution.py:27
  24.1 2.0 collective-permute-done.8
  26.1 1.1 pad_maximum_fusion.4
  27.7 1.5 collective-permute-start.10
  29.2 3.4 collective-permute-done.3
  32.6 1.0 collective-permute-done.2
  33.6 2.1 pad_maximum_fusion.3
  36.2 1.5 collective-permute-start.4
  37.8 18.6 %collective-permute-done.11 = f32[3,3,1,33152]{3,2,1,0:T(1,128)S(1)} collective-permute-done((f32[3,3,1,33152]{3,2,1,0:T(1,128)S(1)}, f32[3,3,1,33152]{3,2,1,0:T(1,128)S(1)}, u32[]{:S(2)}, u32[]{:S(2)}) %collective-permute-start.11) | collective-permute-done | bytes 1193504 | tf_op jit(solution)/shard_map/ppermute | solution.py:27
  56.3 25.6 %collective-permute-done.10 = f32[3,3,1,33152]{3,2,1,0:T(1,128)S(1)} collective-permute-done((f32[3,3,1,33152]{3,2,1,0:T(1,128)S(1)}, f32[3,3,1,33152]{3,2,1,0:T(1,128)S(1)}, u32[]{:S(2)}, u32[]{:S(2)}) %collective-permute-start.10) | collective-permute-done | bytes 1193504 | tf_op jit(solution)/shard_map/ppermute | solution.py:25
  81.9 4.6 %pad_maximum_fusion.2 = f32[3,3,3,33152]{3,2,1,0:T(4,128)} fusion(f32[3,3,1,33152]{3,2,1,0:T(1,128)S(1)} %collective-permute-done.11, f32[3,1,1,33152]{3,2,1,0:T(1,128)S(1)} %collective-permute-done.9, f32[3,1,1,33152]{3,2,1,0:T(1,128)S(1)} %constant_dynamic-update-slice_fusion.3, f32[3,1,1,33152]{3,2,1,0:T(1,128)S(1)} %collective-permute-done.8, ...), kind=kLoop, calls=%fused_computation.31 | loop fusion | flops 3580416 | bytes 7160832 | tf_op jit(solution)/shard_map/concatenate | solution.py:23
  86.5 7.8 %reshape.84 = f32[27,33152]{1,0:T(8,128)} reshape(f32[3,3,3,33152]{3,2,1,0:T(4,128)} %pad_maximum_fusion.2) | data formatting | bytes 7160832 | tf_op jit(solution)/shard_map/reshape | solution.py:93
  94.4 13.1 %collective-permute-done.5 = f32[3,3,1,33152]{3,2,1,0:T(1,128)S(1)} collective-permute-done((f32[3,3,1,33152]{3,2,1,0:T(1,128)}, f32[3,3,1,33152]{3,2,1,0:T(1,128)S(1)}, u32[]{:S(2)}, u32[]{:S(2)}) %collective-permute-start.5) | collective-permute-done | bytes 1193504 | tf_op jit(solution)/shard_map/ppermute | solution.py:27
  107.5 22.9 %collective-permute-done.4 = f32[3,3,1,33152]{3,2,1,0:T(1,128)} collective-permute-done((f32[3,3,1,33152]{3,2,1,0:T(1,128)}, f32[3,3,1,33152]{3,2,1,0:T(1,128)}, u32[]{:S(2)}, u32[]{:S(2)}) %collective-permute-start.4) | collective-permute-done | bytes 1193504 | tf_op jit(solution)/shard_map/ppermute | solution.py:25
  130.4 5.8 %pad_maximum_fusion.1 = f32[3,3,3,33152]{3,2,1,0:T(4,128)} fusion(f32[3,3,1,33152]{3,2,1,0:T(1,128)S(1)} %collective-permute-done.5, f32[3,1,1,33152]{3,2,1,0:T(1,128)S(1)} %collective-permute-done.3, f32[3,1,1,33152]{3,2,1,0:T(1,128)S(1)} %constant_dynamic-update-slice_fusion, f32[3,1,1,33152]{3,2,1,0:T(1,128)S(1)} %collective-permute-done.2, ...), kind=kLoop, calls=%fused_computation.30 | loop fusion | flops 3580416 | bytes 7160832 | tf_op jit(solution)/shard_map/concatenate | solution.py:23
  136.1 8.0 %reshape.80 = f32[27,33152]{1,0:T(8,128)} reshape(f32[3,3,3,33152]{3,2,1,0:T(4,128)} %pad_maximum_fusion.1) | data formatting | bytes 7160832 | tf_op jit(solution)/shard_map/reshape | solution.py:93
  144.1 4.6 %slice.46 = f32[27,32768]{1,0:T(8,128)} slice(f32[27,33152]{1,0:T(8,128)} %reshape.80), slice={[0:27], [0:32768]} | slice | bytes 7077888 | tf_op jit(solution)/shard_map/slice | solution.py:94
  148.7 1.3 copy.11
  150.0 2.1 slice.49
  152.1 3.5 copy.10
  155.6 2.1 slice.48
  158.4 6.7 %pad_maximum_fusion = f32[27,256,256]{2,1,0:T(8,128)} fusion(f32[27,128,256]{2,1,0:T(8,128)} %slice.49, f32[27,128,256]{2,1,0:T(8,128)} %slice.48), kind=kLoop, calls=%fused_computation.29 | loop fusion | flops 1769472 | bytes 14155776 | tf_op jit(solution)/shard_map/concatenate | solution.py:109
  165.2 194.3 %while.44 = (s32[]{:T(128)}, f32[256,256]{1,0:T(8,128)S(1)}, s32[27]{0:T(128)S(1)}, s32[]{:T(128)}, f32[27,3,256]{2,1,0:T(4,128)S(1)}, /*index=5*/f32[27,256,256...) while((s32[]{:T(128)}, f32[256,256]{1,0:T(8,128)S(1)}, ...), condition=%wide.region_6.7_spmd, body=%wide.region_2.6_spmd.sunk | while | flops 403751360 | bytes 1598066 | solution.py:130
  168.9 2.8 while.45
  174.4 1.0 dynamic-slice_bitcast_fusion.5
  175.4 2.8 while.45
  180.9 1.0 dynamic-slice_bitcast_fusion.5
  181.9 2.8 while.45
  188.4 2.8 while.45
  193.9 1.0 dynamic-slice_bitcast_fusion.5
  194.8 2.8 while.45
  201.3 2.8 while.45
  206.8 1.0 dynamic-slice_bitcast_fusion.5
  207.8 5.5 %while.45 = (s32[]{:T(128)}, f32[256,256]{1,0:T(8,128)S(1)}, s32[]{:T(128)}, s32[]{:T(128)}, s32[]{:T(128)}, /*index=5*/pred[]{:T(512)}, s32[]{:T(128)}, f32[3,2...) while((s32[]{:T(128)}, f32[256,256]{1,0:T(8,128)S(1)}, ...), condition=%wide.region_5.5_spmd, body=%wide.region_3.4_spmd.sunk | while | flops 403751328 | bytes 1066960 | solution.py:80
  217.0 2.8 while.45
  223.5 5.5 %while.45 = (s32[]{:T(128)}, f32[256,256]{1,0:T(8,128)S(1)}, s32[]{:T(128)}, s32[]{:T(128)}, s32[]{:T(128)}, /*index=5*/pred[]{:T(512)}, s32[]{:T(128)}, f32[3,2...) while((s32[]{:T(128)}, f32[256,256]{1,0:T(8,128)S(1)}, ...), condition=%wide.region_5.5_spmd, body=%wide.region_3.4_spmd.sunk | while | flops 403751328 | bytes 1066960 | solution.py:80
  232.8 5.5 %while.45 = (s32[]{:T(128)}, f32[256,256]{1,0:T(8,128)S(1)}, s32[]{:T(128)}, s32[]{:T(128)}, s32[]{:T(128)}, /*index=5*/pred[]{:T(512)}, s32[]{:T(128)}, f32[3,2...) while((s32[]{:T(128)}, f32[256,256]{1,0:T(8,128)S(1)}, ...), condition=%wide.region_5.5_spmd, body=%wide.region_3.4_spmd.sunk | while | flops 403751328 | bytes 1066960 | solution.py:80
  241.0 1.0 dynamic-slice_bitcast_fusion.5
  242.0 2.8 while.45
  247.5 1.0 dynamic-slice_bitcast_fusion.5
  248.5 5.5 %while.45 = (s32[]{:T(128)}, f32[256,256]{1,0:T(8,128)S(1)}, s32[]{:T(128)}, s32[]{:T(128)}, s32[]{:T(128)}, /*index=5*/pred[]{:T(512)}, s32[]{:T(128)}, f32[3,2...) while((s32[]{:T(128)}, f32[256,256]{1,0:T(8,128)S(1)}, ...), condition=%wide.region_5.5_spmd, body=%wide.region_3.4_spmd.sunk | while | flops 403751328 | bytes 1066960 | solution.py:80
  256.8 1.0 dynamic-slice_bitcast_fusion.5
  257.7 2.8 while.45
  263.2 1.0 dynamic-slice_bitcast_fusion.5
  264.2 5.5 %while.45 = (s32[]{:T(128)}, f32[256,256]{1,0:T(8,128)S(1)}, s32[]{:T(128)}, s32[]{:T(128)}, s32[]{:T(128)}, /*index=5*/pred[]{:T(512)}, s32[]{:T(128)}, f32[3,2...) while((s32[]{:T(128)}, f32[256,256]{1,0:T(8,128)S(1)}, ...), condition=%wide.region_5.5_spmd, body=%wide.region_3.4_spmd.sunk | while | flops 403751328 | bytes 1066960 | solution.py:80
  273.5 2.8 while.45
  279.9 5.5 %while.45 = (s32[]{:T(128)}, f32[256,256]{1,0:T(8,128)S(1)}, s32[]{:T(128)}, s32[]{:T(128)}, s32[]{:T(128)}, /*index=5*/pred[]{:T(512)}, s32[]{:T(128)}, f32[3,2...) while((s32[]{:T(128)}, f32[256,256]{1,0:T(8,128)S(1)}, ...), condition=%wide.region_5.5_spmd, body=%wide.region_3.4_spmd.sunk | while | flops 403751328 | bytes 1066960 | solution.py:80
  289.2 2.8 while.45
  295.7 5.5 %while.45 = (s32[]{:T(128)}, f32[256,256]{1,0:T(8,128)S(1)}, s32[]{:T(128)}, s32[]{:T(128)}, s32[]{:T(128)}, /*index=5*/pred[]{:T(512)}, s32[]{:T(128)}, f32[3,2...) while((s32[]{:T(128)}, f32[256,256]{1,0:T(8,128)S(1)}, ...), condition=%wide.region_5.5_spmd, body=%wide.region_3.4_spmd.sunk | while | flops 403751328 | bytes 1066960 | solution.py:80
  304.9 2.8 while.45
  311.4 2.8 while.45
  317.9 2.8 while.45
  324.4 2.8 while.45
  330.8 2.8 while.45
  337.3 2.8 while.45
  343.8 2.8 while.45
  350.3 2.8 while.45
  356.8 2.8 while.45
  359.6 1.1 fusion.20
  (557 shorter events, 130.0 us)
Async XLA Ops:
  0.0 1.4 copy-start
  3.0 11.4 %collective-permute-start.7 = (f32[1,1,1,33152]{3,2,1,0:T(1,128)S(1)}, f32[1,1,1,33152]{3,2,1,0:T(1,128)S(1)}, u32[]{:S(2)}, u32[]{:S(2)}) collective-permute-start(f32[1,1,1,33152]{3,2,1,0:T(1,128)S(1)} %broadcast_in_dim.41), channel_id=1, source_target_pairs={{8,0},{16,8},{24,16},{0,24},{9,1},{17,9},{25,17},{1,25},{10,2},{18... | collective-permute-start | bytes 397832 | tf_op jit(solution)/shard_map/ppermute | solution.py:27
  3.5 10.8 %collective-permute-start.6 = (f32[1,1,1,33152]{3,2,1,0:T(1,128)S(1)}, f32[1,1,1,33152]{3,2,1,0:T(1,128)S(1)}, u32[]{:S(2)}, u32[]{:S(2)}) collective-permute-start(f32[1,1,1,33152]{3,2,1,0:T(1,128)S(1)} %broadcast_in_dim.41), channel_id=1, source_target_pairs={{0,8},{8,16},{16,24},{24,0},{1,9},{9,17},{17,25},{25,1},{2,10},{10... | collective-permute-start | bytes 397832 | tf_op jit(solution)/shard_map/ppermute | solution.py:25
  5.2 13.8 %collective-permute-start.1 = (f32[1,1,1,33152]{3,2,1,0:T(1,128)S(1)}, f32[1,1,1,33152]{3,2,1,0:T(1,128)S(1)}, u32[]{:S(2)}, u32[]{:S(2)}) collective-permute-start(f32[1,1,1,33152]{3,2,1,0:T(1,128)S(1)} %broadcast_in_dim.40), channel_id=1, source_target_pairs={{8,0},{16,8},{24,16},{0,24},{9,1},{17,9},{25,17},{1,25},{10,2},{18... | collective-permute-start | bytes 397832 | tf_op jit(solution)/shard_map/ppermute | solution.py:27
  7.3 11.6 %collective-permute-start = (f32[1,1,1,33152]{3,2,1,0:T(1,128)S(1)}, f32[1,1,1,33152]{3,2,1,0:T(1,128)S(1)}, u32[]{:S(2)}, u32[]{:S(2)}) collective-permute-start(f32[1,1,1,33152]{3,2,1,0:T(1,128)S(1)} %broadcast_in_dim.40), channel_id=1, source_target_pairs={{0,8},{8,16},{16,24},{24,0},{1,9},{9,17},{17,25},{25,1},{2,10},{10... | collective-permute-start | bytes 397832 | tf_op jit(solution)/shard_map/ppermute | solution.py:25
  14.5 9.6 %collective-permute-start.9 = (f32[3,1,1,33152]{3,2,1,0:T(1,128)S(1)}, f32[3,1,1,33152]{3,2,1,0:T(1,128)S(1)}, u32[]{:S(2)}, u32[]{:S(2)}) collective-permute-start(f32[3,1,1,33152]{3,2,1,0:T(1,128)S(1)} %constant_dynamic-update-slice_fusion.3), channel_id=1, source_target_pairs={{2,0},{4,2},{6,4},{0,6},{3,1},{5,3},{7,5},{1,7},{10,8},{12,10},{14... | collective-permute-start | bytes 1193480 | tf_op jit(solution)/shard_map/ppermute | solution.py:27
  14.5 11.6 %collective-permute-start.8 = (f32[3,1,1,33152]{3,2,1,0:T(1,128)S(1)}, f32[3,1,1,33152]{3,2,1,0:T(1,128)S(1)}, u32[]{:S(2)}, u32[]{:S(2)}) collective-permute-start(f32[3,1,1,33152]{3,2,1,0:T(1,128)S(1)} %constant_dynamic-update-slice_fusion.3), channel_id=1, source_target_pairs={{0,2},{2,4},{4,6},{6,0},{1,3},{3,5},{5,7},{7,1},{8,10},{10,12},{12... | collective-permute-start | bytes 1193480 | tf_op jit(solution)/shard_map/ppermute | solution.py:25
  19.1 13.6 %collective-permute-start.3 = (f32[3,1,1,33152]{3,2,1,0:T(1,128)S(1)}, f32[3,1,1,33152]{3,2,1,0:T(1,128)S(1)}, u32[]{:S(2)}, u32[]{:S(2)}) collective-permute-start(f32[3,1,1,33152]{3,2,1,0:T(1,128)S(1)} %constant_dynamic-update-slice_fusion), channel_id=1, source_target_pairs={{2,0},{4,2},{6,4},{0,6},{3,1},{5,3},{7,5},{1,7},{10,8},{12,10},{14... | collective-permute-start | bytes 1193480 | tf_op jit(solution)/shard_map/ppermute | solution.py:27
  19.1 14.5 %collective-permute-start.2 = (f32[3,1,1,33152]{3,2,1,0:T(1,128)S(1)}, f32[3,1,1,33152]{3,2,1,0:T(1,128)S(1)}, u32[]{:S(2)}, u32[]{:S(2)}) collective-permute-start(f32[3,1,1,33152]{3,2,1,0:T(1,128)S(1)} %constant_dynamic-update-slice_fusion), channel_id=1, source_target_pairs={{0,2},{2,4},{4,6},{6,0},{1,3},{3,5},{5,7},{7,1},{8,10},{10,12},{12... | collective-permute-start | bytes 1193480 | tf_op jit(solution)/shard_map/ppermute | solution.py:25
  27.1 29.2 %collective-permute-start.11 = (f32[3,3,1,33152]{3,2,1,0:T(1,128)S(1)}, f32[3,3,1,33152]{3,2,1,0:T(1,128)S(1)}, u32[]{:S(2)}, u32[]{:S(2)}) collective-permute-start(f32[3,3,1,33152]{3,2,1,0:T(1,128)S(1)} %pad_maximum_fusion.4), channel_id=1, source_target_pairs={{1,0},{0,1},{3,2},{2,3},{5,4},{4,5},{7,6},{6,7},{9,8},{8,9},{11,10... | collective-permute-start | bytes 3580424 | tf_op jit(solution)/shard_map/ppermute | solution.py:27
  27.7 54.2 %collective-permute-start.10 = (f32[3,3,1,33152]{3,2,1,0:T(1,128)S(1)}, f32[3,3,1,33152]{3,2,1,0:T(1,128)S(1)}, u32[]{:S(2)}, u32[]{:S(2)}) collective-permute-start(f32[3,3,1,33152]{3,2,1,0:T(1,128)S(1)} %pad_maximum_fusion.4), channel_id=1, source_target_pairs={{0,1},{1,0},{2,3},{3,2},{4,5},{5,4},{6,7},{7,6},{8,9},{9,8},{10,11... | collective-permute-start | bytes 3580424 | tf_op jit(solution)/shard_map/ppermute | solution.py:25
  35.7 71.8 %collective-permute-start.5 = (f32[3,3,1,33152]{3,2,1,0:T(1,128)}, f32[3,3,1,33152]{3,2,1,0:T(1,128)S(1)}, u32[]{:S(2)}, u32[]{:S(2)}) collective-permute-start(f32[3,3,1,33152]{3,2,1,0:T(1,128)} %pad_maximum_fusion.3), channel_id=1, source_target_pairs={{1,0},{0,1},{3,2},{2,3},{5,4},{4,5},{7,6},{6,7},{9,8},{8,9},{11,10... | collective-permute-start | bytes 3580424 | tf_op jit(solution)/shard_map/ppermute | solution.py:27
  36.2 94.1 %collective-permute-start.4 = (f32[3,3,1,33152]{3,2,1,0:T(1,128)}, f32[3,3,1,33152]{3,2,1,0:T(1,128)}, u32[]{:S(2)}, u32[]{:S(2)}) collective-permute-start(f32[3,3,1,33152]{3,2,1,0:T(1,128)} %pad_maximum_fusion.3), channel_id=1, source_target_pairs={{0,1},{1,0},{2,3},{3,2},{4,5},{5,4},{6,7},{7,6},{8,9},{9,8},{10,11... | collective-permute-start | bytes 3580424 | tf_op jit(solution)/shard_map/ppermute | solution.py:25
  144.1 4.6 %slice-start.1 = ((f32[27,33152]{1,0:T(8,128)}), f32[27,32768]{1,0:T(8,128)S(1)}, s32[]{:S(2)}) async-start(f32[27,33152]{1,0:T(8,128)} %reshape.84), calls=%async_computation.1 | async-start | bytes 8388608 | tf_op jit(solution)/shard_map/slice | solution.py:94
  150.0 2.1 slice-start
  155.6 2.1 slice-start.2
  158.4 6.8 %copy-start.3 = (f32[8,256]{1,0:T(8,128)S(1)}, f32[8,256]{1,0:T(8,128)}, u32[]{:S(2)}) copy-start(f32[8,256]{1,0:T(8,128)} %param.15) | copy-start | bytes 24580
  165.2 194.4 %copy-start.1 = (f32[1,1,1,256,256]{4,3,2,1,0:T(8,128)S(1)}, f32[1,1,1,256,256]{4,3,2,1,0:T(8,128)}, u32[]{:S(2)}) copy-start(f32[1,1,1,256,256]{4,3,2,1,0:T(8,128)} %param.10) | copy-start | bytes 786436
  165.2 194.4 %copy-start.2 = (f32[256,256]{1,0:T(8,128)S(1)}, f32[256,256]{1,0:T(8,128)}, u32[]{:S(2)}) copy-start(f32[256,256]{1,0:T(8,128)} %param.14) | copy-start | bytes 786436
where the time goes:
time: 360 us; the launch traced here: 361 us
  waiting for transfers between devices  101 us (28%)
  local copies, waits for them, and re-layouts  74.7 us (21%)
  loops' own time  62.2 us (17%)
  other arithmetic  56.2 us (16%)
  matrix products  56.1 us (16%)
  starting transfers between devices  9.39 us (3%)
    ppermute x6, waiting for transfers between devices, padded(): lax.ppermute(tail, axis, [(i, (i + 1) % count) for i in range(count)])  61.5 us
    another operation x1, loops' own time, local(): message = lax.fori_loop(0, 27, add_task, running)  54.7 us
    dot_general x68, matrix products, radial_terms(): jnp.dot(radial_basis.reshape(BLK, NRBF * BLK), weighted, precision=highes...  53.7 us
    ppermute x6, waiting for transfers between devices, padded(): lax.ppermute(head, axis, [((i + 1) % count, i) for i in range(count)])  39.6 us
    squeeze x27, local copies, waits for them, and re-layouts, add_task(): near_feats[task_index]  26.3 us
    select_n x68, other arithmetic, radial_terms(): jnp.where(diagonal & same_bin & (row_block == col_block), 0.0, envelope)  18.3 us
    dynamic_slice x27, local copies, waits for them, and re-layouts, add_task(): right_blocks = jnp.where(task_index < skipped, 0, near_blocks[task_index])  16.7 us
    reshape x2, local copies, waits for them, and re-layouts, unpack_bins(): flat = joined.reshape(27, -1)  15.8 us
  transfers between devices with their start and end apart: 12, of which 10 were waited for; matrix products, arithmetic and copies ran while one was open for 5% of the time, Pallas kernels for 0%

commit v1 on v0

v1 whole, which is shorter than its diff:
```python
import math

import jax
import jax.numpy as jnp
import numpy as np
from jax import lax
from jax.experimental import pallas as pl
from jax.experimental.pallas import tpu as pltpu
from jax.sharding import PartitionSpec as P

BLK = 128
CHUNK = 256
far_value = 100.0
gamma_width = 10.0
message_scale = 0.125
highest = lax.Precision.HIGHEST
f32, bf16, i32 = jnp.float32, jnp.bfloat16, jnp.int32


def envelope_coefficients():
    t = np.cos(np.pi * (np.arange(64) + 0.5) / 64) * 0.5 + 0.5
    value = 0.5 * (np.cos(np.pi * np.sqrt(t)) + 1.0)
    fit = np.polynomial.chebyshev.Chebyshev.fit(t, value, 7, domain=[0, 1])
    return [float(c) for c in fit.convert(kind=np.polynomial.Polynomial).coef]


ENVELOPE = envelope_coefficients()


def split(value):
    high = value.astype(bf16)
    return high, (value - high.astype(f32)).astype(bf16)


def dot(a, b):
    return jnp.dot(a, b, preferred_element_type=f32)


def dot3(a, b):
    ah, al = split(a)
    bh, bl = split(b)
    return dot(ah, bh) + (dot(ah, bl) + dot(al, bh))


def project_kernel(feats_ref, place_ref, w_ref, early_ref, later_ref):
    value = dot3(feats_ref[...], w_ref[...])
    early_ref[:BLK] = value[:BLK]
    early_ref[BLK:] = place_ref[...]
    later_ref[...] = value[BLK:]


def pairs_kernel(tiles, mirrored, nrbf, *refs):
    early = refs[:tiles]
    later = refs[tiles : 2 * tiles]
    shift_ref, own_ref, feats_ref, radial_ref, w_ref, out_ref = refs[2 * tiles : 2 * tiles + 6]
    high_p, low_p, where_j, where_i, high_b, low_b, total, message = refs[2 * tiles + 6 :]
    lane = lax.broadcasted_iota(i32, (8, BLK), 1)
    counts = [jnp.max(t[BLK + 3 : BLK + 4, :BLK]).astype(i32) for t in early]
    own_blocks = (counts[0] + BLK - 1) // BLK

    def append(rows_ref, place, count, at):
        rows = (count + 15) // 16 * 16
        high, low = split(rows_ref[:BLK])
        at = pl.multiple_of(at, 16)
        high_p[pl.ds(at, BLK), :] = high
        low_p[pl.ds(at, BLK), :] = low
        turn = lax.rem(at, BLK)
        page = at // BLK
        rolled = pltpu.roll(place, turn, 1)
        where_j[page] = jnp.where(lane >= turn, rolled, where_j[page])
        where_j[page + 1] = rolled
        return at + rows

    at = jnp.int32(0)
    for half, source in ((0, early), (1, later)):
        for t in range(tiles):
            count = own_blocks * BLK if t == 0 else counts[t]
            here = jnp.clip(count - half * BLK, 0, BLK)
            place = early[t][BLK:, half * BLK : (half + 1) * BLK]
            shift = shift_ref[t]
            if half:
                @pl.when(here > 0)
                def _():
                    append(source[t], place + shift, here, at)

                at = at + (here + 15) // 16 * 16
            else:
                at = append(source[t], place + shift, here, at)
            if t == 0 and half == 0 and tiles:
                @pl.when(own_blocks > 1)
                def _():
                    append(later[0], early[0][BLK:, BLK:] + shift_ref[0], jnp.int32(BLK), jnp.int32(BLK))

                at = own_blocks * BLK
                counts[0] = jnp.int32(0)
                own_count = own_blocks
                own_blocks = jnp.int32(0)
    own_blocks = own_count
    tail = pl.multiple_of(at, 16)
    zeros = jnp.zeros((CHUNK, high_p.shape[1]), bf16)
    high_p[pl.ds(tail, CHUNK), :] = zeros
    low_p[pl.ds(tail, CHUNK), :] = zeros
    far = jnp.where(lax.broadcasted_iota(i32, (8, BLK), 0) < 4, 2 * far_value, 0.0)
    page = at // BLK
    where_j[page] = jnp.where(lane >= lax.rem(at, BLK), far, where_j[page])
    where_j[page + 1] = far
    where_j[page + 2] = far
    chunks = (at + CHUNK - 1) // CHUNK
    place_i = own_ref[...]
    difference = lax.broadcasted_iota(i32, (32, BLK), 0) - lax.broadcasted_iota(i32, (32, BLK), 1)

    message[...] = jnp.zeros_like(message)

    @pl.loop(0, own_blocks)
    def _(row_block):
        row = pl.multiple_of(row_block * BLK, BLK)
        mine = own_ref[pl.ds(row, BLK), :]
        for c in range(3):
            where_i[c] = jnp.broadcast_to(mine[:, c : c + 1], (BLK, BLK))
        total[...] = jnp.zeros_like(total)

        @pl.loop(0, chunks)
        def _(chunk):
            for half in range(CHUNK // BLK):
                theirs = where_j[chunk * (CHUNK // BLK) + half]
                gap = chunk * CHUNK + half * BLK - row
                for sub in range(0, BLK, 32):
                    square = None
                    for c in range(3):
                        delta = theirs[c : c + 1, :] - where_i[c, sub : sub + 32, :]
                        if mirrored[c]:
                            delta = theirs[c + 4 : c + 5, :] - jnp.abs(delta)
                        delta = delta * delta
                        square = delta if square is None else square + delta
                    reach = (square < 1.0) & (difference != gap - sub)
                    square = jnp.minimum(square, 1.0)
                    distance = square * lax.rsqrt(jnp.maximum(square, 1e-30))
                    envelope = jnp.full_like(square, ENVELOPE[-1])
                    for coefficient in ENVELOPE[-2::-1]:
                        envelope = envelope * square + coefficient
                    envelope = jnp.where(reach, envelope, 0.0)
                    step = gamma_width / nrbf
                    basis = envelope * jnp.exp(step * distance - gamma_width * square)
                    ratio = jnp.exp(2.0 * step * distance)
                    for k in range(nrbf):
                        if k:
                            basis = basis * ratio
                        high, low = split(basis)
                        spot = (slice(k * BLK + sub, k * BLK + sub + 32), slice(half * BLK, half * BLK + BLK))
                        high_b[spot] = high
                        low_b[spot] = low
            base = pl.multiple_of(chunk * CHUNK, CHUNK)
            ph = high_p[pl.ds(base, CHUNK), :]
            pw = low_p[pl.ds(base, CHUNK), :]
            bh = high_b[...]
            total[...] += dot(bh, ph) + (dot(bh, pw) + dot(low_b[...], ph))

        value = None
        for k in range(nrbf):
            weight = radial_ref[k : k + 1, :] * math.exp(-gamma_width * ((k + 0.5) / nrbf) ** 2)
            term = total[k * BLK : (k + 1) * BLK, :] * weight
            value = term if value is None else value + term
        message[pl.ds(row, BLK), :] = value * message_scale

    mixed = dot3(message[...], w_ref[...])
    out_ref[...] = feats_ref[...] + mixed / (1.0 + jnp.exp(-mixed))


def exchange(values, axis, pairs):
    return [tuple(lax.ppermute(v, axis, pairs) for v in value) for value in values]


def near_tiles(own, names):
    ax, ay, az = names
    tiles = [(own, [0, 0, 0], [0, 0, 0])]

    def moved(which, dim, pairs, offset, mirror):
        arrays = exchange([w[0] for w in which], names[dim], pairs)
        found = []
        for a, (_, o, m) in zip(arrays, which):
            o, m = list(o), list(m)
            if mirror:
                m[dim] = 1
            else:
                o[dim] = offset
            found.append((a, o, m))
        return found

    def grow(which, dim):
        n = lax.axis_size(names[dim])
        if n == 2:
            return moved(which, dim, [(0, 1), (1, 0)], 0, True)
        up = [(i, (i + 1) % n) for i in range(n)]
        down = [((i + 1) % n, i) for i in range(n)]
        return moved(which, dim, up, -1, False) + moved(which, dim, down, 1, False)

    n = lax.axis_size(ay)
    paired = n > 2 and n % 2 == 0
    if paired:
        side = 1 - 2 * lax.rem(lax.axis_index(ay), 2)
        cross = [(i, (i - 1) % n if i % 2 == 0 else (i + 1) % n) for i in range(n)]
        partner = [(i, i ^ 1) for i in range(n)]
        tiles = tiles + moved(tiles, 1, cross, -side, False)
    else:
        tiles = tiles + grow(tiles, 1)
    tiles = tiles + grow(tiles, 2)
    tiles = tiles + grow(tiles, 0)
    if paired:
        middle = [t for t in tiles if isinstance(t[1][1], int) and t[1][1] == 0]
        tiles = tiles + moved(middle, 1, partner, side, False)
    return tiles


def local(features, positions, counts, w_src, w_out, radial):
    feats = features[0, 0, 0]
    cap, width = feats.shape
    nrbf = radial.shape[0]
    slot = lax.broadcasted_iota(i32, (1, cap), 1)
    count = counts[0, 0, 0]
    placed = jnp.where(slot < count, positions[0, 0, 0], far_value)
    place = jnp.concatenate([placed, jnp.broadcast_to(count.astype(f32), (1, cap)), jnp.zeros((4, cap), f32)])
    names = ("gx", "gy", "gz")
    early, later = pl.pallas_call(
        project_kernel,
        out_shape=(jax.ShapeDtypeStruct((BLK + 8, width), f32), jax.ShapeDtypeStruct((cap - BLK, width), f32)),
    )(feats, place, w_src)
    tiles = near_tiles((early, later), names)
    total = len(tiles)
    mirrored = tuple(lax.axis_size(n) == 2 for n in names)
    rows = []
    for _, offset, mirror in tiles:
        rows += [*offset, 0, *mirror, 0]
    shift = jnp.stack([jnp.asarray(r, f32) for r in rows]).reshape(total, 8, 1)
    shift = jnp.broadcast_to(shift, (total, 8, BLK))
    own = jnp.concatenate([placed.T, jnp.zeros((cap, 5), f32)], axis=1)
    room = total * cap + 2 * CHUNK
    out = pl.pallas_call(
        lambda *refs: pairs_kernel(total, mirrored, nrbf, *refs),
        out_shape=jax.ShapeDtypeStruct((cap, width), f32),
        scratch_shapes=[
            pltpu.VMEM((room, width), bf16),
            pltpu.VMEM((room, width), bf16),
            pltpu.VMEM((room // BLK + 2, 8, BLK), f32),
            pltpu.VMEM((3, BLK, BLK), f32),
            pltpu.VMEM((nrbf * BLK, CHUNK), bf16),
            pltpu.VMEM((nrbf * BLK, CHUNK), bf16),
            pltpu.VMEM((nrbf * BLK, width), f32),
            pltpu.VMEM((cap, width), f32),
        ],
        compiler_params=pltpu.CompilerParams(vmem_limit_bytes=56 << 20),
    )(*[t[0][0] for t in tiles], *[t[0][1] for t in tiles], shift, own, feats, radial, w_out)
    return out[None, None, None]


def solution(mesh):
    in_specs = (P("gx", "gy", "gz", None, None), P("gx", "gy", "gz", None, None), P("gx", "gy", "gz"), P(), P(), P())
    return jax.shard_map(local, mesh=mesh, in_specs=in_specs, out_specs=P("gx", "gy", "gz", None, None), check_vma=False)
```

time: 360 us -> 86.2 us (0.24)
  the two profiles are of different devices: /device:TPU:14 before, /device:TPU:20 now
where the time goes in v1:
time: 86.2 us; the launch traced here: 86.7 us
  waiting for transfers between devices  33.4 us (39%)
  starting transfers between devices  26.2 us (30%)
  Pallas kernels  22.6 us (26%)
  local copies, waits for them, and re-layouts  2.62 us (3%)
  between operations  1.03 us (1%)
  other arithmetic  0.89 us (1%)
    ppermute x34, waiting for transfers between devices, exchange(): lax.ppermute(v, axis, pairs)  33.4 us
    ppermute x34, starting transfers between devices, exchange(): lax.ppermute(v, axis, pairs)  26.2 us
    pallas_call x1, Pallas kernels, local(): pl.pallas_call(lambda *refs: pairs_kernel(total, mirrored, nrbf, *refs),...  20.6 us
    pallas_call x1, Pallas kernels, local(): pl.pallas_call(project_kernel, out_shape=(jax.ShapeDtypeStruct((BLK + 8,...  1.99 us
  transfers between devices with their start and end apart: 34, of which 15 were waited for; matrix products, arithmetic and copies ran while one was open for 1% of the time, Pallas kernels for 0%

profile of v1, /device:TPU:20, one launch (start us, length us, event | category | flops | bytes accessed | tf_op | source)
XLA Modules:
  0.0 86.7 jit_solution(1649334461896266295)
XLA Ops:
  0.7 0.0 copy-start.30
  0.7 0.1 pad.2.clone
  0.8 0.1 pad.3.clone
  0.8 0.5 copy-done.30
  1.4 0.1 copy.9
  1.5 0.1 bitcast_select_fusion
  1.6 0.1 copy.10
  1.7 0.7 maximum_maximum_fusion.place_ref
  2.4 2.0 %shard_map.64 = (f32[136,256]{1,0:T(8,128)}, f32[128,256]{1,0:T(8,128)}) custom-call(f32[256,256]{1,0:T(8,128)} %bitcast.14, f32[8,256]{1,0:T(8,128)} %maximum_maximum_fusion.place_ref, f32[256,256]{1,0:T(8,128)} %w_ref.1), custom_call_target="tpu_custom_call" | custom-call | tf_op jit(solution)/shard_map/pallas_call | solution.py:223
  4.4 0.4 collective-permute-start.24
  4.8 1.6 %collective-permute-start.20 = (f32[128,256]{1,0:T(8,128)}, f32[128,256]{1,0:T(8,128)S(1)}, u32[]{:S(2)}, u32[]{:S(2)}) collective-permute-start(f32[128,256]{1,0:T(8,128)} %get-tuple-element.8.refs_18_), channel_id=1, source_target_pairs={{0,8},{8,16},{16,24},{24,0},{1,9},{9,17},{17,25},{25,1},{2,10},{10... | collective-permute-start | bytes 393224 | tf_op jit(solution)/shard_map/ppermute | solution.py:170
  6.4 0.5 collective-permute-start.18
  6.9 0.8 collective-permute-start.17
  7.7 0.8 collective-permute-start.11
  8.5 2.0 %collective-permute-done.24.refs_26_ = f32[128,256]{1,0:T(8,128)S(1)} collective-permute-done((f32[128,256]{1,0:T(8,128)}, f32[128,256]{1,0:T(8,128)S(1)}, u32[]{:S(2)}, u32[]{:S(2)}) %collective-permute-start.24) | collective-permute-done | bytes 131104 | tf_op jit(solution)/shard_map/ppermute | solution.py:170
  10.5 0.4 collective-permute-start.7
  10.9 2.5 %collective-permute-done.20.refs_22_ = f32[128,256]{1,0:T(8,128)S(1)} collective-permute-done((f32[128,256]{1,0:T(8,128)}, f32[128,256]{1,0:T(8,128)S(1)}, u32[]{:S(2)}, u32[]{:S(2)}) %collective-permute-start.20) | collective-permute-done | bytes 131104 | tf_op jit(solution)/shard_map/ppermute | solution.py:170
  13.5 1.6 %collective-permute-start.3 = (f32[136,256]{1,0:T(8,128)}, f32[136,256]{1,0:T(8,128)S(1)}, u32[]{:S(2)}, u32[]{:S(2)}) collective-permute-start(f32[136,256]{1,0:T(8,128)} %get-tuple-element.7.refs_0_), channel_id=1, source_target_pairs={{0,8},{8,16},{16,24},{24,0},{1,9},{9,17},{17,25},{25,1},{2,10},{10... | collective-permute-start | bytes 417800 | tf_op jit(solution)/shard_map/ppermute | solution.py:170
  15.0 0.5 collective-permute-start.1
  15.6 0.0 collective-permute-done.11.refs_12_
  15.6 1.6 %collective-permute-start.32 = (f32[128,256]{1,0:T(8,128)S(1)}, f32[128,256]{1,0:T(8,128)S(1)}, u32[]{:S(2)}, u32[]{:S(2)}) collective-permute-start(f32[128,256]{1,0:T(8,128)S(1)} %collective-permute-done.24.refs_26_), channel_id=1, source_target_pairs={{0,2},{2,0},{4,6},{6,4},{1,3},{3,1},{5,7},{7,5},{8,10},{10,8},{12,... | collective-permute-start | bytes 393224 | tf_op jit(solution)/shard_map/ppermute | solution.py:170
  17.2 0.4 collective-permute-done.7.refs_8_
  17.6 0.0 collective-permute-start.30
  17.6 4.9 %collective-permute-done.3.refs_4_ = f32[136,256]{1,0:T(8,128)S(1)} collective-permute-done((f32[136,256]{1,0:T(8,128)}, f32[136,256]{1,0:T(8,128)S(1)}, u32[]{:S(2)}, u32[]{:S(2)}) %collective-permute-start.3) | collective-permute-done | bytes 139296 | tf_op jit(solution)/shard_map/ppermute | solution.py:170
  22.5 0.0 collective-permute-done.1.refs_2_
  22.5 0.8 collective-permute-start.26
  23.3 1.5 %collective-permute-start.22 = (f32[128,256]{1,0:T(8,128)S(1)}, f32[128,256]{1,0:T(8,128)S(1)}, u32[]{:S(2)}, u32[]{:S(2)}) collective-permute-start(f32[128,256]{1,0:T(8,128)S(1)} %collective-permute-done.18.refs_20_), channel_id=1, source_target_pairs={{0,8},{8,16},{16,24},{24,0},{1,9},{9,17},{17,25},{25,1},{2,10},{10... | collective-permute-start | bytes 393224 | tf_op jit(solution)/shard_map/ppermute | solution.py:170
  24.8 0.0 collective-permute-done.32.refs_34_
  24.8 0.5 collective-permute-start.25
  25.4 0.0 collective-permute-done.29.refs_31_
  25.4 2.1 %collective-permute-start.21 = (f32[128,256]{1,0:T(8,128)S(1)}, f32[128,256]{1,0:T(8,128)S(1)}, u32[]{:S(2)}, u32[]{:S(2)}) collective-permute-start(f32[128,256]{1,0:T(8,128)S(1)} %collective-permute-done.17.refs_19_), channel_id=1, source_target_pairs={{0,8},{8,16},{16,24},{24,0},{1,9},{9,17},{17,25},{25,1},{2,10},{10... | collective-permute-start | bytes 393224 | tf_op jit(solution)/shard_map/ppermute | solution.py:170
  27.5 1.4 %collective-permute-done.26.refs_28_ = f32[128,256]{1,0:T(8,128)S(1)} collective-permute-done((f32[128,256]{1,0:T(8,128)S(1)}, f32[128,256]{1,0:T(8,128)S(1)}, u32[]{:S(2)}, u32[]{:S(2)}) %collective-permute-start.26) | collective-permute-done | bytes 131104 | tf_op jit(solution)/shard_map/ppermute | solution.py:170
  28.9 0.5 collective-permute-start.19
  29.4 3.7 %collective-permute-done.22.refs_24_ = f32[128,256]{1,0:T(8,128)S(1)} collective-permute-done((f32[128,256]{1,0:T(8,128)S(1)}, f32[128,256]{1,0:T(8,128)S(1)}, u32[]{:S(2)}, u32[]{:S(2)}) %collective-permute-start.22) | collective-permute-done | bytes 131104 | tf_op jit(solution)/shard_map/ppermute | solution.py:170
  33.1 0.0 collective-permute-start.13
  33.1 1.5 %collective-permute-done.25.refs_27_ = f32[128,256]{1,0:T(8,128)S(1)} collective-permute-done((f32[128,256]{1,0:T(8,128)S(1)}, f32[128,256]{1,0:T(8,128)S(1)}, u32[]{:S(2)}, u32[]{:S(2)}) %collective-permute-start.25) | collective-permute-done | bytes 131104 | tf_op jit(solution)/shard_map/ppermute | solution.py:170
  34.6 2.7 %collective-permute-done.21.refs_23_ = f32[128,256]{1,0:T(8,128)S(1)} collective-permute-done((f32[128,256]{1,0:T(8,128)S(1)}, f32[128,256]{1,0:T(8,128)S(1)}, u32[]{:S(2)}, u32[]{:S(2)}) %collective-permute-start.21) | collective-permute-done | bytes 131104 | tf_op jit(solution)/shard_map/ppermute | solution.py:170
  37.3 1.1 %collective-permute-start.9 = (f32[136,256]{1,0:T(8,128)S(1)}, f32[136,256]{1,0:T(8,128)S(1)}, u32[]{:S(2)}, u32[]{:S(2)}) collective-permute-start(f32[136,256]{1,0:T(8,128)S(1)} %collective-permute-done.1.refs_2_), channel_id=1, source_target_pairs={{8,0},{16,8},{24,16},{0,24},{9,1},{17,9},{25,17},{1,25},{10,2},{18... | collective-permute-start | bytes 417800 | tf_op jit(solution)/shard_map/ppermute | solution.py:170
  38.4 0.0 collective-permute-done.19.refs_21_
  38.5 0.9 %collective-permute-start.5 = (f32[136,256]{1,0:T(8,128)S(1)}, f32[136,256]{1,0:T(8,128)S(1)}, u32[]{:S(2)}, u32[]{:S(2)}) collective-permute-start(f32[136,256]{1,0:T(8,128)S(1)} %collective-permute-done.1.refs_2_), channel_id=1, source_target_pairs={{0,8},{8,16},{16,24},{24,0},{1,9},{9,17},{17,25},{25,1},{2,10},{10... | collective-permute-start | bytes 417800 | tf_op jit(solution)/shard_map/ppermute | solution.py:170
  39.4 0.0 collective-permute-done.15.refs_16_
  39.4 1.1 %collective-permute-start.8 = (f32[136,256]{1,0:T(8,128)S(1)}, f32[136,256]{1,0:T(8,128)S(1)}, u32[]{:S(2)}, u32[]{:S(2)}) collective-permute-start(f32[136,256]{1,0:T(8,128)S(1)} %collective-permute-done.refs_1_), channel_id=1, source_target_pairs={{8,0},{16,8},{24,16},{0,24},{9,1},{17,9},{25,17},{1,25},{10,2},{18... | collective-permute-start | bytes 417800 | tf_op jit(solution)/shard_map/ppermute | solution.py:170
  40.5 0.0 collective-permute-done.13.refs_14_
  40.5 2.2 %collective-permute-start.4 = (f32[136,256]{1,0:T(8,128)S(1)}, f32[136,256]{1,0:T(8,128)S(1)}, u32[]{:S(2)}, u32[]{:S(2)}) collective-permute-start(f32[136,256]{1,0:T(8,128)S(1)} %collective-permute-done.refs_1_), channel_id=1, source_target_pairs={{0,8},{8,16},{16,24},{24,0},{1,9},{9,17},{17,25},{25,1},{2,10},{10... | collective-permute-start | bytes 417800 | tf_op jit(solution)/shard_map/ppermute | solution.py:170
  42.7 0.0 collective-permute-done.12.refs_13_
  42.7 1.1 %collective-permute-start.2 = (f32[136,256]{1,0:T(8,128)S(1)}, f32[136,256]{1,0:T(8,128)S(1)}, u32[]{:S(2)}, u32[]{:S(2)}) collective-permute-start(f32[136,256]{1,0:T(8,128)S(1)} %collective-permute-done.refs_1_), channel_id=1, source_target_pairs={{0,1},{1,0},{2,3},{3,2},{4,5},{5,4},{6,7},{7,6},{8,9},{9,8},{10,11... | collective-permute-start | bytes 417800 | tf_op jit(solution)/shard_map/ppermute | solution.py:170
  43.8 0.6 collective-permute-done.9.refs_10_
  44.4 4.5 %collective-permute-done.5.refs_6_ = f32[136,256]{1,0:T(8,128)S(1)} collective-permute-done((f32[136,256]{1,0:T(8,128)S(1)}, f32[136,256]{1,0:T(8,128)S(1)}, u32[]{:S(2)}, u32[]{:S(2)}) %collective-permute-start.5) | collective-permute-done | bytes 139296 | tf_op jit(solution)/shard_map/ppermute | solution.py:170
  48.9 1.1 %collective-permute-done.8.refs_9_ = f32[136,256]{1,0:T(8,128)S(1)} collective-permute-done((f32[136,256]{1,0:T(8,128)S(1)}, f32[136,256]{1,0:T(8,128)S(1)}, u32[]{:S(2)}, u32[]{:S(2)}) %collective-permute-start.8) | collective-permute-done | bytes 139296 | tf_op jit(solution)/shard_map/ppermute | solution.py:170
  50.0 0.2 collective-permute-start.27
  50.2 0.2 stack.8
  50.4 0.1 broadcast_in_dim.33
  50.5 1.5 %collective-permute-done.4.refs_5_ = f32[136,256]{1,0:T(8,128)S(1)} collective-permute-done((f32[136,256]{1,0:T(8,128)S(1)}, f32[136,256]{1,0:T(8,128)S(1)}, u32[]{:S(2)}, u32[]{:S(2)}) %collective-permute-start.4) | collective-permute-done | bytes 139296 | tf_op jit(solution)/shard_map/ppermute | solution.py:170
  52.0 1.4 %collective-permute-start.23 = (f32[128,256]{1,0:T(8,128)}, f32[128,256]{1,0:T(8,128)S(1)}, u32[]{:S(2)}, u32[]{:S(2)}) collective-permute-start(f32[128,256]{1,0:T(8,128)} %collective-permute-done.19.refs_21_), channel_id=1, source_target_pairs={{0,8},{8,16},{16,24},{24,0},{1,9},{9,17},{17,25},{25,1},{2,10},{10... | collective-permute-start | bytes 393224 | tf_op jit(solution)/shard_map/ppermute | solution.py:170
  53.4 0.6 collective-permute-start.10
  54.0 3.3 %collective-permute-start.6 = (f32[136,256]{1,0:T(8,128)S(1)}, f32[136,256]{1,0:T(8,128)S(1)}, u32[]{:S(2)}, u32[]{:S(2)}) collective-permute-start(f32[136,256]{1,0:T(8,128)S(1)} %collective-permute-done.2.refs_3_), channel_id=1, source_target_pairs={{0,8},{8,16},{16,24},{24,0},{1,9},{9,17},{17,25},{25,1},{2,10},{10... | collective-permute-start | bytes 417800 | tf_op jit(solution)/shard_map/ppermute | solution.py:170
  57.3 0.5 collective-permute-start.14
  57.8 0.1 fusion
  58.0 0.7 concatenate.7.refs_37_
  58.6 2.8 %collective-permute-done.23.refs_25_ = f32[128,256]{1,0:T(8,128)S(1)} collective-permute-done((f32[128,256]{1,0:T(8,128)}, f32[128,256]{1,0:T(8,128)S(1)}, u32[]{:S(2)}, u32[]{:S(2)}) %collective-permute-start.23) | collective-permute-done | bytes 131104 | tf_op jit(solution)/shard_map/ppermute | solution.py:170
  61.5 2.0 %collective-permute-done.10.refs_11_ = f32[136,256]{1,0:T(8,128)S(1)} collective-permute-done((f32[136,256]{1,0:T(8,128)S(1)}, f32[136,256]{1,0:T(8,128)S(1)}, u32[]{:S(2)}, u32[]{:S(2)}) %collective-permute-start.10) | collective-permute-done | bytes 139296 | tf_op jit(solution)/shard_map/ppermute | solution.py:170
  63.5 1.6 %collective-permute-done.6.refs_7_ = f32[136,256]{1,0:T(8,128)S(1)} collective-permute-done((f32[136,256]{1,0:T(8,128)S(1)}, f32[136,256]{1,0:T(8,128)S(1)}, u32[]{:S(2)}, u32[]{:S(2)}) %collective-permute-start.6) | collective-permute-done | bytes 139296 | tf_op jit(solution)/shard_map/ppermute | solution.py:170
  65.1 0.7 broadcast_in_dim.34.refs_36_
  66.1 20.6 %shard_map.65 = f32[256,256]{1,0:T(8,128)} custom-call(f32[136,256]{1,0:T(8,128)} %get-tuple-element.7.refs_0_, f32[136,256]{1,0:T(8,128)} %copy-done.4, f32[136,256]{1,0:T(8,128)} %copy-done.3, f32[136,256]{1,0:T(8,128)} %copy-done.12, f32[136,256]{1,0:T(8,128)} %copy-done.2, f32[136,256]{1,0:T(8,128)} %copy-done.11, f32[136,256]{1,0:T(8,128)} %copy-done.9, ...), custom_call_target="tpu_custom_call" | custom-call | tf_op jit(solution)/shard_map/pallas_call | solution.py:237
  (83 shorter events, 0.2 us)
Async XLA Ops:
  4.4 3.3 %collective-permute-start.28 = (f32[128,256]{1,0:T(8,128)}, f32[128,256]{1,0:T(8,128)S(1)}, u32[]{:S(2)}, u32[]{:S(2)}) collective-permute-start(f32[128,256]{1,0:T(8,128)} %get-tuple-element.8.refs_18_), channel_id=1, source_target_pairs={{0,2},{2,0},{4,6},{6,4},{1,3},{3,1},{5,7},{7,5},{8,10},{10,8},{12,... | collective-permute-start | bytes 393224 | tf_op jit(solution)/shard_map/ppermute | solution.py:170
  4.4 6.1 %collective-permute-start.24 = (f32[128,256]{1,0:T(8,128)}, f32[128,256]{1,0:T(8,128)S(1)}, u32[]{:S(2)}, u32[]{:S(2)}) collective-permute-start(f32[128,256]{1,0:T(8,128)} %get-tuple-element.8.refs_18_), channel_id=1, source_target_pairs={{8,0},{16,8},{24,16},{0,24},{9,1},{17,9},{25,17},{1,25},{10,2},{18... | collective-permute-start | bytes 393224 | tf_op jit(solution)/shard_map/ppermute | solution.py:170
  4.8 8.6 %collective-permute-start.20 = (f32[128,256]{1,0:T(8,128)}, f32[128,256]{1,0:T(8,128)S(1)}, u32[]{:S(2)}, u32[]{:S(2)}) collective-permute-start(f32[128,256]{1,0:T(8,128)} %get-tuple-element.8.refs_18_), channel_id=1, source_target_pairs={{0,8},{8,16},{16,24},{24,0},{1,9},{9,17},{17,25},{25,1},{2,10},{10... | collective-permute-start | bytes 393224 | tf_op jit(solution)/shard_map/ppermute | solution.py:170
  6.4 8.7 %collective-permute-start.18 = (f32[128,256]{1,0:T(8,128)}, f32[128,256]{1,0:T(8,128)S(1)}, u32[]{:S(2)}, u32[]{:S(2)}) collective-permute-start(f32[128,256]{1,0:T(8,128)} %get-tuple-element.8.refs_18_), channel_id=1, source_target_pairs={{0,1},{1,0},{2,3},{3,2},{4,5},{5,4},{6,7},{7,6},{8,9},{9,8},{10,11... | collective-permute-start | bytes 393224 | tf_op jit(solution)/shard_map/ppermute | solution.py:170
  6.9 8.7 %collective-permute-start.17 = (f32[128,256]{1,0:T(8,128)}, f32[128,256]{1,0:T(8,128)S(1)}, u32[]{:S(2)}, u32[]{:S(2)}) collective-permute-start(f32[128,256]{1,0:T(8,128)} %get-tuple-element.8.refs_18_), channel_id=1, source_target_pairs={{0,6},{2,4},{4,2},{6,0},{1,7},{3,5},{5,3},{7,1},{8,14},{10,12},{12... | collective-permute-start | bytes 393224 | tf_op jit(solution)/shard_map/ppermute | solution.py:170
  7.7 58.2 %copy-start.17 = (f32[128,256]{1,0:T(8,128)}, f32[128,256]{1,0:T(8,128)S(1)}, u32[]{:S(2)}) copy-start(f32[128,256]{1,0:T(8,128)S(1)} %collective-permute-done.28.refs_30_) | copy-start | bytes 393220
  7.7 7.9 %collective-permute-start.11 = (f32[136,256]{1,0:T(8,128)}, f32[136,256]{1,0:T(8,128)S(1)}, u32[]{:S(2)}, u32[]{:S(2)}) collective-permute-start(f32[136,256]{1,0:T(8,128)} %get-tuple-element.7.refs_0_), channel_id=1, source_target_pairs={{0,2},{2,0},{4,6},{6,4},{1,3},{3,1},{5,7},{7,5},{8,10},{10,8},{12,... | collective-permute-start | bytes 417800 | tf_op jit(solution)/shard_map/ppermute | solution.py:170
  10.5 55.4 %copy-start.18 = (f32[128,256]{1,0:T(8,128)}, f32[128,256]{1,0:T(8,128)S(1)}, u32[]{:S(2)}) copy-start(f32[128,256]{1,0:T(8,128)S(1)} %collective-permute-done.24.refs_26_) | copy-start | bytes 393220
  10.5 7.1 %collective-permute-start.7 = (f32[136,256]{1,0:T(8,128)}, f32[136,256]{1,0:T(8,128)S(1)}, u32[]{:S(2)}, u32[]{:S(2)}) collective-permute-start(f32[136,256]{1,0:T(8,128)} %get-tuple-element.7.refs_0_), channel_id=1, source_target_pairs={{8,0},{16,8},{24,16},{0,24},{9,1},{17,9},{25,17},{1,25},{10,2},{18... | collective-permute-start | bytes 417800 | tf_op jit(solution)/shard_map/ppermute | solution.py:170
  13.5 52.4 %copy-start.19 = (f32[128,256]{1,0:T(8,128)}, f32[128,256]{1,0:T(8,128)S(1)}, u32[]{:S(2)}) copy-start(f32[128,256]{1,0:T(8,128)S(1)} %collective-permute-done.20.refs_22_) | copy-start | bytes 393220
  13.5 9.0 %collective-permute-start.3 = (f32[136,256]{1,0:T(8,128)}, f32[136,256]{1,0:T(8,128)S(1)}, u32[]{:S(2)}, u32[]{:S(2)}) collective-permute-start(f32[136,256]{1,0:T(8,128)} %get-tuple-element.7.refs_0_), channel_id=1, source_target_pairs={{0,8},{8,16},{16,24},{24,0},{1,9},{9,17},{17,25},{25,1},{2,10},{10... | collective-permute-start | bytes 417800 | tf_op jit(solution)/shard_map/ppermute | solution.py:170
  15.0 50.8 %copy-start.20 = (f32[128,256]{1,0:T(8,128)}, f32[128,256]{1,0:T(8,128)S(1)}, u32[]{:S(2)}) copy-start(f32[128,256]{1,0:T(8,128)S(1)} %collective-permute-done.18.refs_20_) | copy-start | bytes 393220
  15.0 7.5 %collective-permute-start.1 = (f32[136,256]{1,0:T(8,128)}, f32[136,256]{1,0:T(8,128)S(1)}, u32[]{:S(2)}, u32[]{:S(2)}) collective-permute-start(f32[136,256]{1,0:T(8,128)} %get-tuple-element.7.refs_0_), channel_id=1, source_target_pairs={{0,1},{1,0},{2,3},{3,2},{4,5},{5,4},{6,7},{7,6},{8,9},{9,8},{10,11... | collective-permute-start | bytes 417800 | tf_op jit(solution)/shard_map/ppermute | solution.py:170
  15.6 50.3 %copy-start.21 = (f32[128,256]{1,0:T(8,128)}, f32[128,256]{1,0:T(8,128)S(1)}, u32[]{:S(2)}) copy-start(f32[128,256]{1,0:T(8,128)S(1)} %collective-permute-done.17.refs_19_) | copy-start | bytes 393220
  15.6 7.8 %collective-permute-start = (f32[136,256]{1,0:T(8,128)}, f32[136,256]{1,0:T(8,128)S(1)}, u32[]{:S(2)}, u32[]{:S(2)}) collective-permute-start(f32[136,256]{1,0:T(8,128)} %get-tuple-element.7.refs_0_), channel_id=1, source_target_pairs={{0,6},{2,4},{4,2},{6,0},{1,7},{3,5},{5,3},{7,1},{8,14},{10,12},{12... | collective-permute-start | bytes 417800 | tf_op jit(solution)/shard_map/ppermute | solution.py:170
  15.6 42.4 %copy-start = (f32[136,256]{1,0:T(8,128)}, f32[136,256]{1,0:T(8,128)S(1)}, u32[]{:S(2)}) copy-start(f32[136,256]{1,0:T(8,128)S(1)} %collective-permute-done.11.refs_12_) | copy-start | bytes 417796
  15.6 9.2 %collective-permute-start.32 = (f32[128,256]{1,0:T(8,128)S(1)}, f32[128,256]{1,0:T(8,128)S(1)}, u32[]{:S(2)}, u32[]{:S(2)}) collective-permute-start(f32[128,256]{1,0:T(8,128)S(1)} %collective-permute-done.24.refs_26_), channel_id=1, source_target_pairs={{0,2},{2,0},{4,6},{6,4},{1,3},{3,1},{5,7},{7,5},{8,10},{10,8},{12,... | collective-permute-start | bytes 393224 | tf_op jit(solution)/shard_map/ppermute | solution.py:170
  17.6 40.3 %copy-start.1 = (f32[136,256]{1,0:T(8,128)}, f32[136,256]{1,0:T(8,128)S(1)}, u32[]{:S(2)}) copy-start(f32[136,256]{1,0:T(8,128)S(1)} %collective-permute-done.7.refs_8_) | copy-start | bytes 417796
  17.6 7.8 %collective-permute-start.30 = (f32[128,256]{1,0:T(8,128)S(1)}, f32[128,256]{1,0:T(8,128)S(1)}, u32[]{:S(2)}, u32[]{:S(2)}) collective-permute-start(f32[128,256]{1,0:T(8,128)S(1)} %collective-permute-done.20.refs_22_), channel_id=1, source_target_pairs={{0,2},{2,0},{4,6},{6,4},{1,3},{3,1},{5,7},{7,5},{8,10},{10,8},{12,... | collective-permute-start | bytes 393224 | tf_op jit(solution)/shard_map/ppermute | solution.py:170
  22.5 43.4 %copy-start.2 = (f32[136,256]{1,0:T(8,128)}, f32[136,256]{1,0:T(8,128)S(1)}, u32[]{:S(2)}) copy-start(f32[136,256]{1,0:T(8,128)S(1)} %collective-permute-done.3.refs_4_) | copy-start | bytes 417796
  22.5 2.9 %collective-permute-start.29 = (f32[128,256]{1,0:T(8,128)S(1)}, f32[128,256]{1,0:T(8,128)S(1)}, u32[]{:S(2)}, u32[]{:S(2)}) collective-permute-start(f32[128,256]{1,0:T(8,128)S(1)} %collective-permute-done.18.refs_20_), channel_id=1, source_target_pairs={{0,2},{2,0},{4,6},{6,4},{1,3},{3,1},{5,7},{7,5},{8,10},{10,8},{12,... | collective-permute-start | bytes 393224 | tf_op jit(solution)/shard_map/ppermute | solution.py:170
  22.5 43.4 %copy-start.3 = (f32[136,256]{1,0:T(8,128)}, f32[136,256]{1,0:T(8,128)S(1)}, u32[]{:S(2)}) copy-start(f32[136,256]{1,0:T(8,128)S(1)} %collective-permute-done.1.refs_2_) | copy-start | bytes 417796
  22.5 6.4 %collective-permute-start.26 = (f32[128,256]{1,0:T(8,128)S(1)}, f32[128,256]{1,0:T(8,128)S(1)}, u32[]{:S(2)}, u32[]{:S(2)}) collective-permute-start(f32[128,256]{1,0:T(8,128)S(1)} %collective-permute-done.18.refs_20_), channel_id=1, source_target_pairs={{8,0},{16,8},{24,16},{0,24},{9,1},{17,9},{25,17},{1,25},{10,2},{18... | collective-permute-start | bytes 393224 | tf_op jit(solution)/shard_map/ppermute | solution.py:170
  23.3 42.5 %copy-start.4 = (f32[136,256]{1,0:T(8,128)}, f32[136,256]{1,0:T(8,128)S(1)}, u32[]{:S(2)}) copy-start(f32[136,256]{1,0:T(8,128)S(1)} %collective-permute-done.refs_1_) | copy-start | bytes 417796
  23.3 9.7 %collective-permute-start.22 = (f32[128,256]{1,0:T(8,128)S(1)}, f32[128,256]{1,0:T(8,128)S(1)}, u32[]{:S(2)}, u32[]{:S(2)}) collective-permute-start(f32[128,256]{1,0:T(8,128)S(1)} %collective-permute-done.18.refs_20_), channel_id=1, source_target_pairs={{0,8},{8,16},{16,24},{24,0},{1,9},{9,17},{17,25},{25,1},{2,10},{10... | collective-permute-start | bytes 393224 | tf_op jit(solution)/shard_map/ppermute | solution.py:170
  24.8 41.1 %copy-start.22 = (f32[128,256]{1,0:T(8,128)}, f32[128,256]{1,0:T(8,128)S(1)}, u32[]{:S(2)}) copy-start(f32[128,256]{1,0:T(8,128)S(1)} %collective-permute-done.32.refs_34_) | copy-start | bytes 393220
  24.8 9.8 %collective-permute-start.25 = (f32[128,256]{1,0:T(8,128)S(1)}, f32[128,256]{1,0:T(8,128)S(1)}, u32[]{:S(2)}, u32[]{:S(2)}) collective-permute-start(f32[128,256]{1,0:T(8,128)S(1)} %collective-permute-done.17.refs_19_), channel_id=1, source_target_pairs={{8,0},{16,8},{24,16},{0,24},{9,1},{17,9},{25,17},{1,25},{10,2},{18... | collective-permute-start | bytes 393224 | tf_op jit(solution)/shard_map/ppermute | solution.py:170
  25.4 40.5 %copy-start.23 = (f32[128,256]{1,0:T(8,128)}, f32[128,256]{1,0:T(8,128)S(1)}, u32[]{:S(2)}) copy-start(f32[128,256]{1,0:T(8,128)S(1)} %collective-permute-done.30.refs_32_) | copy-start | bytes 393220
  25.4 14.0 %collective-permute-start.15 = (f32[136,256]{1,0:T(8,128)S(1)}, f32[136,256]{1,0:T(8,128)S(1)}, u32[]{:S(2)}, u32[]{:S(2)}) collective-permute-start(f32[136,256]{1,0:T(8,128)S(1)} %collective-permute-done.7.refs_8_), channel_id=1, source_target_pairs={{0,2},{2,0},{4,6},{6,4},{1,3},{3,1},{5,7},{7,5},{8,10},{10,8},{12,... | collective-permute-start | bytes 417800 | tf_op jit(solution)/shard_map/ppermute | solution.py:170
  25.4 40.5 %copy-start.24 = (f32[128,256]{1,0:T(8,128)}, f32[128,256]{1,0:T(8,128)S(1)}, u32[]{:S(2)}) copy-start(f32[128,256]{1,0:T(8,128)S(1)} %collective-permute-done.29.refs_31_) | copy-start | bytes 393220
  25.4 11.9 %collective-permute-start.21 = (f32[128,256]{1,0:T(8,128)S(1)}, f32[128,256]{1,0:T(8,128)S(1)}, u32[]{:S(2)}, u32[]{:S(2)}) collective-permute-start(f32[128,256]{1,0:T(8,128)S(1)} %collective-permute-done.17.refs_19_), channel_id=1, source_target_pairs={{0,8},{8,16},{16,24},{24,0},{1,9},{9,17},{17,25},{25,1},{2,10},{10... | collective-permute-start | bytes 393224 | tf_op jit(solution)/shard_map/ppermute | solution.py:170
  28.9 37.0 %copy-start.25 = (f32[128,256]{1,0:T(8,128)}, f32[128,256]{1,0:T(8,128)S(1)}, u32[]{:S(2)}) copy-start(f32[128,256]{1,0:T(8,128)S(1)} %collective-permute-done.26.refs_28_) | copy-start | bytes 393220
  28.9 9.5 %collective-permute-start.19 = (f32[128,256]{1,0:T(8,128)S(1)}, f32[128,256]{1,0:T(8,128)}, u32[]{:S(2)}, u32[]{:S(2)}) collective-permute-start(f32[128,256]{1,0:T(8,128)S(1)} %collective-permute-done.17.refs_19_), channel_id=1, source_target_pairs={{0,1},{1,0},{2,3},{3,2},{4,5},{5,4},{6,7},{7,6},{8,9},{9,8},{10,11... | collective-permute-start | bytes 393224 | tf_op jit(solution)/shard_map/ppermute | solution.py:170
  33.1 32.8 %copy-start.26 = (f32[128,256]{1,0:T(8,128)}, f32[128,256]{1,0:T(8,128)S(1)}, u32[]{:S(2)}) copy-start(f32[128,256]{1,0:T(8,128)S(1)} %collective-permute-done.22.refs_24_) | copy-start | bytes 393220
  33.1 7.4 %collective-permute-start.13 = (f32[136,256]{1,0:T(8,128)S(1)}, f32[136,256]{1,0:T(8,128)S(1)}, u32[]{:S(2)}, u32[]{:S(2)}) collective-permute-start(f32[136,256]{1,0:T(8,128)S(1)} %collective-permute-done.3.refs_4_), channel_id=1, source_target_pairs={{0,2},{2,0},{4,6},{6,4},{1,3},{3,1},{5,7},{7,5},{8,10},{10,8},{12,... | collective-permute-start | bytes 417800 | tf_op jit(solution)/shard_map/ppermute | solution.py:170
  34.6 31.4 %copy-start.27 = (f32[128,256]{1,0:T(8,128)}, f32[128,256]{1,0:T(8,128)S(1)}, u32[]{:S(2)}) copy-start(f32[128,256]{1,0:T(8,128)S(1)} %collective-permute-done.25.refs_27_) | copy-start | bytes 393220
  34.6 8.1 %collective-permute-start.12 = (f32[136,256]{1,0:T(8,128)S(1)}, f32[136,256]{1,0:T(8,128)S(1)}, u32[]{:S(2)}, u32[]{:S(2)}) collective-permute-start(f32[136,256]{1,0:T(8,128)S(1)} %collective-permute-done.1.refs_2_), channel_id=1, source_target_pairs={{0,2},{2,0},{4,6},{6,4},{1,3},{3,1},{5,7},{7,5},{8,10},{10,8},{12,... | collective-permute-start | bytes 417800 | tf_op jit(solution)/shard_map/ppermute | solution.py:170
  37.3 28.6 %copy-start.28 = (f32[128,256]{1,0:T(8,128)}, f32[128,256]{1,0:T(8,128)S(1)}, u32[]{:S(2)}) copy-start(f32[128,256]{1,0:T(8,128)S(1)} %collective-permute-done.21.refs_23_) | copy-start | bytes 393220
  37.3 7.0 %collective-permute-start.9 = (f32[136,256]{1,0:T(8,128)S(1)}, f32[136,256]{1,0:T(8,128)S(1)}, u32[]{:S(2)}, u32[]{:S(2)}) collective-permute-start(f32[136,256]{1,0:T(8,128)S(1)} %collective-permute-done.1.refs_2_), channel_id=1, source_target_pairs={{8,0},{16,8},{24,16},{0,24},{9,1},{17,9},{25,17},{1,25},{10,2},{18... | collective-permute-start | bytes 417800 | tf_op jit(solution)/shard_map/ppermute | solution.py:170
  38.5 10.5 %collective-permute-start.5 = (f32[136,256]{1,0:T(8,128)S(1)}, f32[136,256]{1,0:T(8,128)S(1)}, u32[]{:S(2)}, u32[]{:S(2)}) collective-permute-start(f32[136,256]{1,0:T(8,128)S(1)} %collective-permute-done.1.refs_2_), channel_id=1, source_target_pairs={{0,8},{8,16},{16,24},{24,0},{1,9},{9,17},{17,25},{25,1},{2,10},{10... | collective-permute-start | bytes 417800 | tf_op jit(solution)/shard_map/ppermute | solution.py:170
  39.4 26.6 %copy-start.5 = (f32[136,256]{1,0:T(8,128)}, f32[136,256]{1,0:T(8,128)S(1)}, u32[]{:S(2)}) copy-start(f32[136,256]{1,0:T(8,128)S(1)} %collective-permute-done.15.refs_16_) | copy-start | bytes 417796
  39.4 10.6 %collective-permute-start.8 = (f32[136,256]{1,0:T(8,128)S(1)}, f32[136,256]{1,0:T(8,128)S(1)}, u32[]{:S(2)}, u32[]{:S(2)}) collective-permute-start(f32[136,256]{1,0:T(8,128)S(1)} %collective-permute-done.refs_1_), channel_id=1, source_target_pairs={{8,0},{16,8},{24,16},{0,24},{9,1},{17,9},{25,17},{1,25},{10,2},{18... | collective-permute-start | bytes 417800 | tf_op jit(solution)/shard_map/ppermute | solution.py:170
  40.5 25.5 %copy-start.6 = (f32[136,256]{1,0:T(8,128)}, f32[136,256]{1,0:T(8,128)S(1)}, u32[]{:S(2)}) copy-start(f32[136,256]{1,0:T(8,128)S(1)} %collective-permute-done.13.refs_14_) | copy-start | bytes 417796
  40.5 11.5 %collective-permute-start.4 = (f32[136,256]{1,0:T(8,128)S(1)}, f32[136,256]{1,0:T(8,128)S(1)}, u32[]{:S(2)}, u32[]{:S(2)}) collective-permute-start(f32[136,256]{1,0:T(8,128)S(1)} %collective-permute-done.refs_1_), channel_id=1, source_target_pairs={{0,8},{8,16},{16,24},{24,0},{1,9},{9,17},{17,25},{25,1},{2,10},{10... | collective-permute-start | bytes 417800 | tf_op jit(solution)/shard_map/ppermute | solution.py:170
  42.7 23.3 %copy-start.7 = (f32[136,256]{1,0:T(8,128)}, f32[136,256]{1,0:T(8,128)S(1)}, u32[]{:S(2)}) copy-start(f32[136,256]{1,0:T(8,128)S(1)} %collective-permute-done.12.refs_13_) | copy-start | bytes 417796
  42.7 10.7 %collective-permute-start.2 = (f32[136,256]{1,0:T(8,128)S(1)}, f32[136,256]{1,0:T(8,128)S(1)}, u32[]{:S(2)}, u32[]{:S(2)}) collective-permute-start(f32[136,256]{1,0:T(8,128)S(1)} %collective-permute-done.refs_1_), channel_id=1, source_target_pairs={{0,1},{1,0},{2,3},{3,2},{4,5},{5,4},{6,7},{7,6},{8,9},{9,8},{10,11... | collective-permute-start | bytes 417800 | tf_op jit(solution)/shard_map/ppermute | solution.py:170
  44.4 21.6 %copy-start.8 = (f32[136,256]{1,0:T(8,128)}, f32[136,256]{1,0:T(8,128)S(1)}, u32[]{:S(2)}) copy-start(f32[136,256]{1,0:T(8,128)S(1)} %collective-permute-done.9.refs_10_) | copy-start | bytes 417796
  44.4 9.7 %collective-permute-start.33 = (f32[128,256]{1,0:T(8,128)S(1)}, f32[128,256]{1,0:T(8,128)}, u32[]{:S(2)}, u32[]{:S(2)}) collective-permute-start(f32[128,256]{1,0:T(8,128)S(1)} %collective-permute-done.26.refs_28_), channel_id=1, source_target_pairs={{0,2},{2,0},{4,6},{6,4},{1,3},{3,1},{5,7},{7,5},{8,10},{10,8},{12,... | collective-permute-start | bytes 393224 | tf_op jit(solution)/shard_map/ppermute | solution.py:170
  48.9 17.1 %copy-start.9 = (f32[136,256]{1,0:T(8,128)}, f32[136,256]{1,0:T(8,128)S(1)}, u32[]{:S(2)}) copy-start(f32[136,256]{1,0:T(8,128)S(1)} %collective-permute-done.5.refs_6_) | copy-start | bytes 417796
  48.9 8.4 %collective-permute-start.31 = (f32[128,256]{1,0:T(8,128)S(1)}, f32[128,256]{1,0:T(8,128)}, u32[]{:S(2)}, u32[]{:S(2)}) collective-permute-start(f32[128,256]{1,0:T(8,128)S(1)} %collective-permute-done.22.refs_24_), channel_id=1, source_target_pairs={{0,2},{2,0},{4,6},{6,4},{1,3},{3,1},{5,7},{7,5},{8,10},{10,8},{12,... | collective-permute-start | bytes 393224 | tf_op jit(solution)/shard_map/ppermute | solution.py:170
  50.0 16.0 %copy-start.10 = (f32[136,256]{1,0:T(8,128)}, f32[136,256]{1,0:T(8,128)S(1)}, u32[]{:S(2)}) copy-start(f32[136,256]{1,0:T(8,128)S(1)} %collective-permute-done.8.refs_9_) | copy-start | bytes 417796
  50.0 7.3 %collective-permute-start.27 = (f32[128,256]{1,0:T(8,128)}, f32[128,256]{1,0:T(8,128)}, u32[]{:S(2)}, u32[]{:S(2)}) collective-permute-start(f32[128,256]{1,0:T(8,128)} %collective-permute-done.19.refs_21_), channel_id=1, source_target_pairs={{8,0},{16,8},{24,16},{0,24},{9,1},{17,9},{25,17},{1,25},{10,2},{18... | collective-permute-start | bytes 393224 | tf_op jit(solution)/shard_map/ppermute | solution.py:170
  52.0 14.0 %copy-start.11 = (f32[136,256]{1,0:T(8,128)}, f32[136,256]{1,0:T(8,128)S(1)}, u32[]{:S(2)}) copy-start(f32[136,256]{1,0:T(8,128)S(1)} %collective-permute-done.4.refs_5_) | copy-start | bytes 417796
  52.0 9.5 %collective-permute-start.23 = (f32[128,256]{1,0:T(8,128)}, f32[128,256]{1,0:T(8,128)S(1)}, u32[]{:S(2)}, u32[]{:S(2)}) collective-permute-start(f32[128,256]{1,0:T(8,128)} %collective-permute-done.19.refs_21_), channel_id=1, source_target_pairs={{0,8},{8,16},{16,24},{24,0},{1,9},{9,17},{17,25},{25,1},{2,10},{10... | collective-permute-start | bytes 393224 | tf_op jit(solution)/shard_map/ppermute | solution.py:170
  53.4 12.6 %copy-start.12 = (f32[136,256]{1,0:T(8,128)}, f32[136,256]{1,0:T(8,128)S(1)}, u32[]{:S(2)}) copy-start(f32[136,256]{1,0:T(8,128)S(1)} %collective-permute-done.2.refs_3_) | copy-start | bytes 417796
  53.4 10.1 %collective-permute-start.10 = (f32[136,256]{1,0:T(8,128)S(1)}, f32[136,256]{1,0:T(8,128)S(1)}, u32[]{:S(2)}, u32[]{:S(2)}) collective-permute-start(f32[136,256]{1,0:T(8,128)S(1)} %collective-permute-done.2.refs_3_), channel_id=1, source_target_pairs={{8,0},{16,8},{24,16},{0,24},{9,1},{17,9},{25,17},{1,25},{10,2},{18... | collective-permute-start | bytes 417800 | tf_op jit(solution)/shard_map/ppermute | solution.py:170
  54.0 11.1 %collective-permute-start.6 = (f32[136,256]{1,0:T(8,128)S(1)}, f32[136,256]{1,0:T(8,128)S(1)}, u32[]{:S(2)}, u32[]{:S(2)}) collective-permute-start(f32[136,256]{1,0:T(8,128)S(1)} %collective-permute-done.2.refs_3_), channel_id=1, source_target_pairs={{0,8},{8,16},{16,24},{24,0},{1,9},{9,17},{17,25},{25,1},{2,10},{10... | collective-permute-start | bytes 417800 | tf_op jit(solution)/shard_map/ppermute | solution.py:170
  57.3 4.2 %collective-permute-start.16 = (f32[136,256]{1,0:T(8,128)S(1)}, f32[136,256]{1,0:T(8,128)S(1)}, u32[]{:S(2)}, u32[]{:S(2)}) collective-permute-start(f32[136,256]{1,0:T(8,128)S(1)} %collective-permute-done.9.refs_10_), channel_id=1, source_target_pairs={{0,2},{2,0},{4,6},{6,4},{1,3},{3,1},{5,7},{7,5},{8,10},{10,8},{12,... | collective-permute-start | bytes 417800 | tf_op jit(solution)/shard_map/ppermute | solution.py:170
  57.3 4.2 %collective-permute-start.14 = (f32[136,256]{1,0:T(8,128)S(1)}, f32[136,256]{1,0:T(8,128)S(1)}, u32[]{:S(2)}, u32[]{:S(2)}) collective-permute-start(f32[136,256]{1,0:T(8,128)S(1)} %collective-permute-done.5.refs_6_), channel_id=1, source_target_pairs={{0,2},{2,0},{4,6},{6,4},{1,3},{3,1},{5,7},{7,5},{8,10},{10,8},{12,... | collective-permute-start | bytes 417800 | tf_op jit(solution)/shard_map/ppermute | solution.py:170
  61.5 4.6 %copy-start.29 = (f32[128,256]{1,0:T(8,128)}, f32[128,256]{1,0:T(8,128)S(1)}, u32[]{:S(2)}) copy-start(f32[128,256]{1,0:T(8,128)S(1)} %collective-permute-done.23.refs_25_) | copy-start | bytes 393220
  61.5 4.6 %copy-start.15 = (f32[136,256]{1,0:T(8,128)}, f32[136,256]{1,0:T(8,128)S(1)}, u32[]{:S(2)}) copy-start(f32[136,256]{1,0:T(8,128)S(1)} %collective-permute-done.16.refs_17_) | copy-start | bytes 417796
  61.5 4.6 %copy-start.16 = (f32[136,256]{1,0:T(8,128)}, f32[136,256]{1,0:T(8,128)S(1)}, u32[]{:S(2)}) copy-start(f32[136,256]{1,0:T(8,128)S(1)} %collective-permute-done.14.refs_15_) | copy-start | bytes 417796
  63.5 2.6 %copy-start.13 = (f32[136,256]{1,0:T(8,128)}, f32[136,256]{1,0:T(8,128)S(1)}, u32[]{:S(2)}) copy-start(f32[136,256]{1,0:T(8,128)S(1)} %collective-permute-done.10.refs_11_) | copy-start | bytes 417796
  65.1 0.9 %copy-start.14 = (f32[136,256]{1,0:T(8,128)}, f32[136,256]{1,0:T(8,128)S(1)}, u32[]{:S(2)}) copy-start(f32[136,256]{1,0:T(8,128)S(1)} %collective-permute-done.6.refs_7_) | copy-start | bytes 417796
  (1 other events, 0.7 us)
